TPU v7x, 32 devices: a whole 2x2x4 slice. The times are simulated.
32 devices in a mesh: row: 16 (over z, x, core), col: 2 (over y).
Axes of the slice: x: 2, y: 2, z: 4, core: 2. Of those that a mesh axis runs over, the one named last changes fastest.
Arguments:
- messages: bfloat16 [32768, 512], P(('row', 'col')), may hold values from -6 to 6
- counts: int32 [512], P(('row', 'col')), may hold values from 16 to 64, as said below
- targets: int32 [32768], P(('row', 'col')), may hold values from 0 to 63
- mirror: int32 [32768], P(('row', 'col')), may hold values from 0 to 63, as said below
- atom_cot: bfloat16 [1024, 256], P(('row', 'col')), may hold values from -24 to 24
- w_self: bfloat16 [512, 512], replicated, may hold values from -0.25 to 0.25
- w_down: bfloat16 [512, 256], replicated, may hold values from -0.25 to 0.25
- w_up: bfloat16 [256, 512], replicated, may hold values from -0.375 to 0.375
- w_mlp: bfloat16 [512, 512], replicated, may hold values from -0.25 to 0.25
- w_out: bfloat16 [512, 256], replicated, may hold values from -0.25 to 0.25
Outputs:
- atoms: bfloat16 [1024, 256], P(('row', 'col'))
- grad_messages: bfloat16 [32768, 512], P(('row', 'col'))
Inputs may be any that keep to these rules, and one draw needn't show every extreme that they name: counts of block (t, c, s) and block (s, c, t) are equal; diagonal blocks s = t hold an even count; in every column every target group has a block of 64 live edges. For slots k below the block's count, mirror is a one-to-one map onto the live slots of the block with target and source groups swapped in the same column, and the mirror of the mirror is k itself (in diagonal blocks no slot is its own mirror); padded slots map to themselves.
All inputs are finite; a program needn't handle non-finite values.
Results may differ from a plain program's by a relative error of at most 0.012.
Values may be sent and summed in bfloat16 or wider, within the bound.
A program may use at most 64 MiB of HBM per device.

v0:
```python
import jax
import jax.numpy as jnp
from jax import lax
from jax.sharding import PartitionSpec as P


def silu_grad(values):
    sigmoid_v = jax.nn.sigmoid(values)
    return sigmoid_v * (1.0 + values * (1.0 - sigmoid_v))


def times_transposed(left, weight):
    return lax.dot_general(
        left, weight, (((1,), (1,)), ((), ())), preferred_element_type=jnp.float32
    )


def on_device(messages, counts, targets, mirror, atom_cot, w_self, w_down, w_up, w_mlp, w_out):
    row_count = lax.axis_size("row")
    col_count = lax.axis_size("col")
    edge_count = messages.shape[0]
    block_size = edge_count // row_count
    atom_rows_dev = atom_cot.shape[0]
    scale_atoms = (atom_rows_dev * col_count / (edge_count * col_count)) ** 0.5
    live_bool = (jnp.arange(block_size, dtype=jnp.int32)[None, :] < counts[:, None]).reshape(-1)
    live_mask = live_bool.astype(jnp.float32)
    rows_mirror = jnp.arange(edge_count, dtype=jnp.int32) // block_size * block_size + mirror
    down = jnp.dot(messages, w_down, preferred_element_type=jnp.float32).astype(jnp.bfloat16)
    received = lax.all_to_all(down, "row", split_axis=0, concat_axis=0, tiled=True)
    mirrored = jnp.take(received, rows_mirror, axis=0)
    pre_act = jnp.dot(messages, w_self, preferred_element_type=jnp.float32) + jnp.dot(
        mirrored, w_up, preferred_element_type=jnp.float32
    )
    first_res = (messages.astype(jnp.float32) + jax.nn.silu(pre_act)).astype(jnp.bfloat16)
    pre_two = jnp.dot(first_res, w_mlp, preferred_element_type=jnp.float32)
    second_res = (first_res.astype(jnp.float32) + jax.nn.silu(pre_two)).astype(jnp.bfloat16)
    out_edge = (
        jnp.dot(second_res, w_out, preferred_element_type=jnp.float32) * live_mask[:, None]
    ).astype(jnp.bfloat16)
    atom_ids = jnp.arange(atom_rows_dev * col_count, dtype=jnp.int32)
    one_hot = ((atom_ids[:, None] == targets[None, :]) & live_bool[None, :]).astype(jnp.bfloat16)
    group_terms = jnp.dot(one_hot, out_edge, preferred_element_type=jnp.float32)
    group_total = lax.psum(group_terms.astype(jnp.bfloat16), "col").astype(jnp.float32)
    atom_sum = lax.dynamic_slice_in_dim(
        group_total, lax.axis_index("col") * atom_rows_dev, atom_rows_dev, 0
    )
    atoms = (atom_sum * scale_atoms).astype(jnp.bfloat16)
    shard_rows = lax.all_gather(atom_cot, "col", axis=0, tiled=True)
    atom_ids = jnp.arange(shard_rows.shape[0], dtype=jnp.int32)
    one_hot = (atom_ids[:, None] == targets[None, :]).astype(jnp.bfloat16)
    picked = lax.dot_general(
        one_hot, shard_rows, (((0,), (0,)), ((), ())), preferred_element_type=jnp.float32
    )
    g_out = (picked * scale_atoms * live_mask[:, None]).astype(jnp.bfloat16)
    g_second = times_transposed(g_out, w_out)
    g_pre2 = (g_second * silu_grad(pre_two)).astype(jnp.bfloat16)
    g_first = g_second + times_transposed(g_pre2, w_mlp)
    g_pre = (g_first * silu_grad(pre_act)).astype(jnp.bfloat16)
    g_mirrored = times_transposed(g_pre, w_up).astype(jnp.bfloat16)
    local_sum = g_first + times_transposed(g_pre, w_self)
    returned = lax.all_to_all(g_mirrored, "row", split_axis=0, concat_axis=0, tiled=True)
    g_down = jnp.take(returned, rows_mirror, axis=0)
    total = local_sum + times_transposed(g_down, w_down)
    return (atoms, total.astype(jnp.bfloat16))


def solution(mesh):
    return jax.shard_map(
        on_device,
        mesh=mesh,
        in_specs=(
            P(("row", "col"), None),
            P(("row", "col")),
            P(("row", "col")),
            P(("row", "col")),
            P(("row", "col"), None),
            P(),
            P(),
            P(),
            P(),
            P(),
        ),
        out_specs=(P(("row", "col"), None), P(("row", "col"), None)),
        check_vma=False,
    )
```

profile of v0, /device:TPU:0, one launch (start us, length us, event | category | flops | bytes accessed | tf_op | source)
XLA Modules:
  0.0 65.2 jit_solution(12487515239438811234)
XLA Ops:
  0.7 2.6 %convolution_convert_fusion.1 = bf16[1024,256]{1,0:T(8,128)(2,1)} fusion(bf16[1024,512]{1,0:T(8,128)(2,1)} %param.12, bf16[512,256]{1,0:T(8,128)(2,1)} %param.18), kind=kOutput, calls=%fused_computation.15 | convolution fusion | flops 268697600 | bytes 1835008 | tf_op jit(solution)/shard_map/dot_general | solution.py:28
  3.3 7.5 %all-to-all-start = ((bf16[16,64,256]{2,1,0:T(8,128)(2,1)}), bf16[16,64,256]{2,1,0:T(8,128)(2,1)S(1)}, u32[]{:S(2)}, u32[]{:S(2)}) async-start(bf16[16,64,256]{2,1,0:T(8,128)(2,1)} %bitcast), calls=%async_computation | async-start | bytes 1048576 | tf_op jit(solution)/shard_map/all_to_all | solution.py:29
  10.8 0.1 iota_compare_fusion.3
  10.9 0.1 lt.37
  11.0 4.4 %all_gather.3 = bf16[64,256]{1,0:T(8,128)(2,1)S(1)} all-gather(bf16[32,256]{1,0:T(8,128)(2,1)S(1)} %copy-done.9), channel_id=1, replica_groups=mesh['row'=16,'col'=2] {'col'}, dimensions={0}, use_global_device_ids=true | all-gather | bytes 49152 | tf_op jit(solution)/shard_map/all_gather | solution.py:48
  15.4 2.0 %fusion.3 = f32[1024,512]{1,0:T(8,128)} fusion(bf16[512,256]{1,0:T(8,128)(2,1)S(1)} %copy-done.8, bf16[64,256]{1,0:T(8,128)(2,1)S(1)} %all_gather.3, f32[1024]{0:T(1024)S(1)} %broadcast_select_fusion, s32[1024]{0:T(1024)S(1)} %copy-done.11), kind=kOutput, calls=%fused_computation.18 | convolution fusion | flops 302579712 | bytes 2400256 | tf_op jit(solution)/shard_map/dot_general | solution.py:13
  17.4 2.0 %fusion.29 = f32[1024,512]{1,0:T(8,128)} fusion(bf16[1024,512]{1,0:T(8,128)(2,1)S(1)} %copy-done.1, bf16[512,512]{1,0:T(8,128)(2,1)S(1)} %copy-done.3), kind=kOutput, calls=%fused_computation.52 | convolution fusion | flops 536870912 | bytes 3670016 | tf_op jit(solution)/shard_map/dot_general | solution.py:31
  19.5 5.6 %all-to-all-done = bf16[16,64,256]{2,1,0:T(8,128)(2,1)S(1)} async-done(((bf16[16,64,256]{2,1,0:T(8,128)(2,1)}), bf16[16,64,256]{2,1,0:T(8,128)(2,1)S(1)}, u32[]{:S(2)}, u32[]{:S(2)}) %all-to-all-start) | async-done | bytes 524320 | tf_op jit(solution)/shard_map/all_to_all | solution.py:29
  25.1 3.9 %gather_fusion = bf16[1024,256]{1,0:T(8,128)(2,1)S(1)} fusion(bf16[1024,256]{1,0:T(8,128)(2,1)S(1)} %bitcast.21, s32[1024]{0:T(1024)S(1)} %broadcast_clamp_fusion), kind=kCustom, calls=%fused_computation.clone | custom fusion | bytes 1052672 | tf_op jit(solution)/shard_map/jit(_take)/gather | solution.py:30
  29.0 2.5 %add_convert_fusion.2 = (bf16[1024,512]{1,0:T(8,128)(2,1)S(1)}, f32[1024,512]{1,0:T(8,128)S(1)}) fusion(bf16[1024,512]{1,0:T(8,128)(2,1)S(1)} %copy-done.1, f32[1024,512]{1,0:T(8,128)} %fusion.29, bf16[256,512]{1,0:T(8,128)(2,1)S(1)} %copy-done.7, bf16[1024,256]{1,0:T(8,128)(2,1)S(1)} %gather_fusion, pred[1024]{0:T(1024)(128)(4,1)S(1)} %compare_and_fusion), kind=kOutput, calls=%fused_computation.7 | convolution fusion | flops 272891904 | bytes 7078912 | tf_op jit(solution)/shard_map/dot_general | solution.py:31
  31.5 0.7 %fusion.30 = f32[1024,512]{1,0:T(8,128)S(1)} fusion(bf16[1024,512]{1,0:T(8,128)(2,1)S(1)} %get-tuple-element.3, bf16[512,512]{1,0:T(8,128)(2,1)S(1)} %copy-done), kind=kOutput, calls=%fused_computation.53 | convolution fusion | flops 536870912 | bytes 3670016 | tf_op jit(solution)/shard_map/dot_general | solution.py:35
  32.2 0.2 copy-done.5
  32.5 1.0 %copy-done.4 = f32[1024,512]{1,0:T(8,128)S(1)} copy-done((f32[1024,512]{1,0:T(8,128)S(1)}, f32[1024,512]{1,0:T(8,128)}, u32[]{:S(2)}) %copy-start.4) | copy-done | bytes 2097176
  33.5 2.9 %multiply_convert_fusion = (bf16[1024,512]{1,0:T(8,128)(2,1)S(1)}, f32[1024,512]{1,0:T(8,128)}) fusion(f32[1024,512]{1,0:T(8,128)S(1)} %get-tuple-element.4, f32[1024,512]{1,0:T(8,128)S(1)} %copy-done.4, bf16[512,512]{1,0:T(8,128)(2,1)S(1)} %copy-done, f32[1024,512]{1,0:T(8,128)S(1)} %fusion.30), kind=kOutput, calls=%fused_computation.3 | convolution fusion | flops 546832384 | bytes 9961472 | tf_op jit(solution)/shard_map/dot_general | solution.py:13
  36.4 1.0 %copy-done.2 = bf16[1024,512]{1,0:T(8,128)(2,1)} copy-done((bf16[1024,512]{1,0:T(8,128)(2,1)}, bf16[1024,512]{1,0:T(8,128)(2,1)S(1)}, u32[]{:S(2)}) %copy-start.2) | copy-done | bytes 1048600
  37.4 1.3 %convolution_convert_fusion = bf16[1024,256]{1,0:T(8,128)(2,1)} fusion(bf16[1024,512]{1,0:T(8,128)(2,1)S(1)} %get-tuple-element.5, bf16[256,512]{1,0:T(8,128)(2,1)S(1)} %copy-done.7), kind=kOutput, calls=%fused_computation.14 | convolution fusion | flops 268697600 | bytes 1835008 | tf_op jit(solution)/shard_map/dot_general | solution.py:13
  38.6 4.2 %all-to-all-start.1 = ((bf16[16,64,256]{2,1,0:T(8,128)(2,1)}), bf16[16,64,256]{2,1,0:T(8,128)(2,1)S(1)}, u32[]{:S(2)}, u32[]{:S(2)}) async-start(bf16[16,64,256]{2,1,0:T(8,128)(2,1)} %bitcast.22), calls=%async_computation.1 | async-start | bytes 1048576 | tf_op jit(solution)/shard_map/all_to_all | solution.py:61
  42.8 2.2 %fusion.4 = bf16[64,256]{1,0:T(8,128)(2,1)S(1)} fusion(bf16[512,256]{1,0:T(8,128)(2,1)S(1)} %copy-done.8, f32[1024,512]{1,0:T(8,128)S(1)} %fusion.30, bf16[1024,512]{1,0:T(8,128)(2,1)} %copy-done.5, f32[1024]{0:T(1024)S(1)} %convert_element_type.56, s32[1024]{0:T(1024)S(1)} %copy-done.11, pred[1024]{0:T(1024)(128)(4,1)S(1)} %lt.37), kind=kOutput, calls=%fused_computation.19 | convolution fusion | flops 306331648 | bytes 3449856 | tf_op jit(solution)/shard_map/dot_general | solution.py:42
  45.0 8.4 %psum.7 = bf16[64,256]{1,0:T(8,128)(2,1)S(1)} all-reduce(bf16[64,256]{1,0:T(8,128)(2,1)S(1)} %fusion.4), channel_id=1, replica_groups=mesh['row'=16,'col'=2] {'col'}, use_global_device_ids=true, to_apply=%region_0.2 | all-reduce | flops 16384 | bytes 65536 | tf_op jit(solution)/shard_map/psum | solution.py:43
  53.4 0.6 multiply_convert_fusion.3
  54.0 2.1 %fusion.31 = f32[1024,512]{1,0:T(8,128)S(1)} fusion(bf16[1024,512]{1,0:T(8,128)(2,1)} %copy-done.2, bf16[512,512]{1,0:T(8,128)(2,1)} %param.17), kind=kOutput, calls=%fused_computation.54 | convolution fusion | flops 536870912 | bytes 3670016 | tf_op jit(solution)/shard_map/dot_general | solution.py:13
  56.1 1.0 %all-to-all-done.1 = bf16[16,64,256]{2,1,0:T(8,128)(2,1)S(1)} async-done(((bf16[16,64,256]{2,1,0:T(8,128)(2,1)}), bf16[16,64,256]{2,1,0:T(8,128)(2,1)S(1)}, u32[]{:S(2)}, u32[]{:S(2)}) %all-to-all-start.1) | async-done | bytes 524320 | tf_op jit(solution)/shard_map/all_to_all | solution.py:61
  57.1 5.0 %gather_fusion.1 = bf16[1024,256]{1,0:T(8,128)(2,1)} fusion(bf16[1024,256]{1,0:T(8,128)(2,1)S(1)} %bitcast.20, s32[1024]{0:T(1024)S(1)} %broadcast_clamp_fusion), kind=kCustom, calls=%fused_computation.1.clone | custom fusion | bytes 1052672 | tf_op jit(solution)/shard_map/jit(_take)/gather | solution.py:62
  62.0 3.2 %add_convert_fusion = bf16[1024,512]{1,0:T(8,128)(2,1)} fusion(f32[1024,512]{1,0:T(8,128)} %get-tuple-element.6, f32[1024,512]{1,0:T(8,128)S(1)} %fusion.31, bf16[512,256]{1,0:T(8,128)(2,1)S(1)} %copy-done.6, bf16[1024,256]{1,0:T(8,128)(2,1)} %gather_fusion.1, pred[1024]{0:T(1024)(128)(4,1)S(1)} %compare_and_fusion), kind=kOutput, calls=%fused_computation.2 | convolution fusion | flops 270270464 | bytes 6030336 | tf_op jit(solution)/shard_map/dot_general | solution.py:13
  (27 shorter events, 0.1 us)
Async XLA Ops:
  0.6 30.9 %copy-start = (bf16[512,512]{1,0:T(8,128)(2,1)S(1)}, bf16[512,512]{1,0:T(8,128)(2,1)}, u32[]{:S(2)}) copy-start(bf16[512,512]{1,0:T(8,128)(2,1)} %param.20) | copy-start | bytes 1572868
  0.6 10.1 %copy-start.10 = (s32[1024]{0:T(1024)S(1)}, s32[1024]{0:T(1024)}, u32[]{:S(2)}) copy-start(s32[1024]{0:T(1024)} %param.15) | copy-start | bytes 12292
  0.7 10.2 %copy-start.12 = (s32[16]{0:T(128)S(1)}, s32[16]{0:T(128)}, u32[]{:S(2)}) copy-start(s32[16]{0:T(128)} %param.13) | copy-start | bytes 196
  0.7 10.3 %copy-start.9 = (bf16[32,256]{1,0:T(8,128)(2,1)S(1)}, bf16[32,256]{1,0:T(8,128)(2,1)}, u32[]{:S(2)}) copy-start(bf16[32,256]{1,0:T(8,128)(2,1)} %param.16) | copy-start | bytes 49156
  0.7 14.7 %copy-start.8 = (bf16[512,256]{1,0:T(8,128)(2,1)S(1)}, bf16[512,256]{1,0:T(8,128)(2,1)}, u32[]{:S(2)}) copy-start(bf16[512,256]{1,0:T(8,128)(2,1)} %param.21) | copy-start | bytes 786436
  0.7 14.7 %copy-start.11 = (s32[1024]{0:T(1024)S(1)}, s32[1024]{0:T(1024)}, u32[]{:S(2)}) copy-start(s32[1024]{0:T(1024)} %param.14) | copy-start | bytes 12292
  3.3 14.2 %copy-start.1 = (bf16[1024,512]{1,0:T(8,128)(2,1)S(1)}, bf16[1024,512]{1,0:T(8,128)(2,1)}, u32[]{:S(2)}) copy-start(bf16[1024,512]{1,0:T(8,128)(2,1)} %param.12) | copy-start | bytes 3145732
  3.3 14.2 %copy-start.3 = (bf16[512,512]{1,0:T(8,128)(2,1)S(1)}, bf16[512,512]{1,0:T(8,128)(2,1)}, u32[]{:S(2)}) copy-start(bf16[512,512]{1,0:T(8,128)(2,1)} %param.17) | copy-start | bytes 1572868
  3.3 21.8 %all-to-all-start = ((bf16[16,64,256]{2,1,0:T(8,128)(2,1)}), bf16[16,64,256]{2,1,0:T(8,128)(2,1)S(1)}, u32[]{:S(2)}, u32[]{:S(2)}) async-start(bf16[16,64,256]{2,1,0:T(8,128)(2,1)} %bitcast), calls=%async_computation | async-start | bytes 1048576 | tf_op jit(solution)/shard_map/all_to_all | solution.py:29
  25.1 3.9 %copy-start.7 = (bf16[256,512]{1,0:T(8,128)(2,1)S(1)}, bf16[256,512]{1,0:T(8,128)(2,1)}, u32[]{:S(2)}) copy-start(bf16[256,512]{1,0:T(8,128)(2,1)} %param.19) | copy-start | bytes 786436
  31.5 1.0 %copy-start.5 = (bf16[1024,512]{1,0:T(8,128)(2,1)}, bf16[1024,512]{1,0:T(8,128)(2,1)S(1)}, u32[]{:S(2)}) copy-start(bf16[1024,512]{1,0:T(8,128)(2,1)S(1)} %get-tuple-element.3) | copy-start | bytes 3145732
  31.5 2.0 %copy-start.4 = (f32[1024,512]{1,0:T(8,128)S(1)}, f32[1024,512]{1,0:T(8,128)}, u32[]{:S(2)}) copy-start(f32[1024,512]{1,0:T(8,128)} %fusion.3) | copy-start | bytes 6291460
  36.4 1.0 %copy-start.2 = (bf16[1024,512]{1,0:T(8,128)(2,1)}, bf16[1024,512]{1,0:T(8,128)(2,1)S(1)}, u32[]{:S(2)}) copy-start(bf16[1024,512]{1,0:T(8,128)(2,1)S(1)} %get-tuple-element.5) | copy-start | bytes 3145732
  38.6 18.4 %all-to-all-start.1 = ((bf16[16,64,256]{2,1,0:T(8,128)(2,1)}), bf16[16,64,256]{2,1,0:T(8,128)(2,1)S(1)}, u32[]{:S(2)}, u32[]{:S(2)}) async-start(bf16[16,64,256]{2,1,0:T(8,128)(2,1)} %bitcast.22), calls=%async_computation.1 | async-start | bytes 1048576 | tf_op jit(solution)/shard_map/all_to_all | solution.py:61
  57.1 5.0 %copy-start.6 = (bf16[512,256]{1,0:T(8,128)(2,1)S(1)}, bf16[512,256]{1,0:T(8,128)(2,1)}, u32[]{:S(2)}) copy-start(bf16[512,256]{1,0:T(8,128)(2,1)} %param.18) | copy-start | bytes 786436
where the time goes:
time: 65.8 us; the launch traced here: 65.2 us
  matrix products  21.4 us (33%)
  blocking collectives  12.8 us (19%)
  starting transfers between devices  11.7 us (18%)
  local copies, waits for them, and re-layouts  11.2 us (17%)
  waiting for transfers between devices  6.59 us (10%)
  between operations  0.83 us (1%)
  other arithmetic  0.72 us (1%)
    dot_general x5, matrix products, times_transposed(): lax.dot_general(left, weight, (((1,), (1,)), ((), ())), preferred_element...  11.5 us
    psum x1, blocking collectives, on_device(): lax.psum(group_terms.astype(jnp.bfloat16), 'col').astype(jnp.float32)  8.37 us
    all_to_all x1, starting transfers between devices, on_device(): lax.all_to_all(down, 'row', split_axis=0, concat_axis=0, tiled=True)  7.51 us
    all_to_all x1, waiting for transfers between devices, on_device(): lax.all_to_all(down, 'row', split_axis=0, concat_axis=0, tiled=True)  5.61 us
    gather x1, local copies, waits for them, and re-layouts, on_device(): g_down = jnp.take(returned, rows_mirror, axis=0)  4.95 us
    all_gather x1, blocking collectives, on_device(): shard_rows = lax.all_gather(atom_cot, 'col', axis=0, tiled=True)  4.4 us
    all_to_all x1, starting transfers between devices, on_device(): lax.all_to_all(g_mirrored, 'row', split_axis=0, concat_axis=0, tiled=True)  4.16 us
    gather x1, local copies, waits for them, and re-layouts, on_device(): mirrored = jnp.take(received, rows_mirror, axis=0)  3.93 us
  transfers between devices with their start and end apart: 2, of which 2 were waited for; matrix products, arithmetic and copies ran while one was open for 14% of the time, Pallas kernels for 0%

commit v1 on v0

v1 whole, which is shorter than its diff:
```python
import functools

import jax
import jax.numpy as jnp
from jax import lax
from jax.experimental import pallas as pl
from jax.experimental.pallas import tpu as pltpu
from jax.sharding import PartitionSpec as P

MESH = pl.DeviceIdType.MESH
F32 = jnp.float32
BF16 = jnp.bfloat16


def dot_nn(left, right):
    return jnp.dot(left, right, preferred_element_type=F32)


def dot_nt(left, right):
    return lax.dot_general(left, right, (((1,), (1,)), ((), ())), preferred_element_type=F32)


def dot_tn(left, right):
    return lax.dot_general(left, right, (((0,), (0,)), ((), ())), preferred_element_type=F32)


def sigmoid(values):
    return 0.5 + 0.5 * jnp.tanh(0.5 * values)


def partner_of(own, step, count):
    if count & (count - 1):
        return lax.rem(own + step, count)
    result = 0
    bit = 1
    while bit < count:
        mine = (own // bit) % 2
        other = (step // bit) % 2
        result = result + bit * (mine + other - 2 * mine * other)
        bit *= 2
    return result


def kernel(
    rows, cols, group, scale,
    messages, counts, targets, mirror, cot, w_self, w_down, w_up, w_mlp, w_out,
    atoms_out, grad_out,
    msg_v, targets_v, mirror_v, counts_s, cot_all, w_self_v, w_down_v, w_up_v, w_mlp_v, w_out_v,
    send_f, recv_f, send_b, recv_b, local_v, second_v, gsec_v, gpre_v, grad_v, atom_acc, atom_send, atom_recv, atoms_v,
    in_sems, out_sems, sf_sem, rf_sem, sb_sem, rb_sem, cot_ss, cot_rs, at_ss, at_rs,
):
    row = lax.axis_index("row")
    col = lax.axis_index("col")
    edge_count, _ = msg_v.shape
    block = edge_count // rows
    chunks = rows // group
    size = block * group
    atom_dev = cot.shape[0]
    atom_group = atom_dev * cols
    my_chunk = row // group
    my_in = lax.rem(row, group)

    barrier = pltpu.get_barrier_semaphore()
    for off in range(1, rows):
        pl.semaphore_signal(barrier, inc=1, device_id=(lax.rem(row + off, rows), col), device_id_type=MESH)
    for off in range(1, cols):
        pl.semaphore_signal(barrier, inc=1, device_id=(row, lax.rem(col + off, cols)), device_id_type=MESH)

    own_cot = cot_all.at[pl.ds(pl.multiple_of(col * atom_dev, atom_dev), atom_dev)]
    loads = [
        pltpu.make_async_copy(src, dst, in_sems.at[i])
        for i, (src, dst) in enumerate(
            [
                (w_down, w_down_v), (messages, msg_v), (cot, own_cot), (targets, targets_v), (counts, counts_s),
                (w_self, w_self_v), (w_out, w_out_v), (mirror, mirror_v), (w_up, w_up_v), (w_mlp, w_mlp_v),
            ]
        )
    ]
    for load in loads:
        load.start()

    def rows_of(index, length):
        return pl.ds(pl.multiple_of(index * length, length), length)

    def block_copy(src, dst, s_sems, r_sems, src_block, dst_block, sem):
        return pltpu.make_async_remote_copy(
            src_ref=src.at[rows_of(src_block, block)],
            dst_ref=dst.at[rows_of(dst_block, block)],
            send_sem=s_sems.at[src_block],
            recv_sem=r_sems.at[sem],
            device_id=(src_block, col),
            device_id_type=MESH,
        )

    def send_chunk(src, dst, s_sems, r_sems, chunk, last):
        for j in range(group - 1, -1, -1):
            other = chunk * group + partner_of(my_in, j, group)
            if j == 0:
                @pl.when(jnp.logical_not(last))
                def _():
                    block_copy(src, dst, s_sems, r_sems, other, row, row).start()
            else:
                block_copy(src, dst, s_sems, r_sems, other, row, row).start()

    def wait_chunk(src, dst, s_sems, r_sems, chunk, last):
        for j in range(group - 1, -1, -1):
            other = chunk * group + partner_of(my_in, j, group)
            if j == 0:
                @pl.when(jnp.logical_not(last))
                def _():
                    block_copy(src, dst, s_sems, r_sems, other, other, other).wait_recv()
            else:
                block_copy(src, dst, s_sems, r_sems, other, other, other).wait_recv()

    def wait_sent(src, dst, s_sems, r_sems, chunk, last):
        for j in range(group - 1, -1, -1):
            other = chunk * group + partner_of(my_in, j, group)
            if j == 0:
                @pl.when(jnp.logical_not(last))
                def _():
                    block_copy(src, dst, s_sems, r_sems, other, row, row).wait_send()
            else:
                block_copy(src, dst, s_sems, r_sems, other, row, row).wait_send()

    def chunk_at(p):
        return partner_of(my_chunk, chunks - 1 - p, chunks) if not chunks & (chunks - 1) else partner_of(my_chunk, p + 1, chunks)

    loads[0].wait()
    loads[1].wait()

    @pl.loop(0, chunks)
    def _(p):
        rows_c = rows_of(chunk_at(p), size)
        send_f[rows_c, :] = dot_nn(msg_v[rows_c, :], w_down_v[...]).astype(BF16)

    own_rows = rows_of(row, block)
    recv_f[own_rows, :] = send_f[own_rows, :]
    loads[2].wait()
    pl.semaphore_wait(barrier, rows + cols - 2)

    @pl.loop(0, chunks)
    def _(p):
        send_chunk(send_f, recv_f, sf_sem, rf_sem, chunk_at(p), p == chunks - 1)

    def cot_copy(off, owner):
        peer = lax.rem(col + off, cols)
        part = rows_of(owner, atom_dev)
        return pltpu.make_async_remote_copy(
            src_ref=cot_all.at[part],
            dst_ref=cot_all.at[part],
            send_sem=cot_ss.at[off],
            recv_sem=cot_rs.at[owner],
            device_id=(row, peer),
            device_id_type=MESH,
        )

    for off in range(1, cols):
        cot_copy(off, col).start()

    for load in loads[3:]:
        load.wait()

    @pl.loop(0, chunks)
    def _(p):
        rows_c = rows_of(chunk_at(p), size)
        local_v[rows_c, :] = dot_nn(msg_v[rows_c, :], w_self_v[...])

    for off in range(1, cols):
        cot_copy(off, lax.rem(col + off, cols)).wait_recv()
    for off in range(1, cols):
        cot_copy(off, col).wait_send()
    table = (cot_all[...].astype(F32) * scale).astype(BF16)

    def one_hot_of(chunk):
        lanes = lax.broadcasted_iota(jnp.int32, (1, size), 1)
        bound = jnp.zeros((1, size), jnp.int32)
        for j in range(group):
            bound = jnp.where(lanes // block == j, counts_s[chunk * group + j], bound)
        live = lax.rem(lanes, block) < bound
        wanted = jnp.where(live, targets_v[pl.ds(chunk, 1), :], -1)
        ids = lax.broadcasted_iota(jnp.int32, (atom_group, size), 0)
        return jnp.where(ids == wanted, 1.0, 0.0).astype(BF16)

    def mirror_of(chunk):
        lanes = lax.broadcasted_iota(jnp.int32, (1, size), 1)
        wanted = lanes // block * block + mirror_v[pl.ds(chunk, 1), :]
        ids = lax.broadcasted_iota(jnp.int32, (size, size), 0)
        return jnp.where(ids == wanted, 1.0, 0.0).astype(BF16)

    @pl.loop(0, chunks)
    def _(p):
        chunk = chunk_at(p)
        rows_c = rows_of(chunk, size)
        g_out = dot_tn(one_hot_of(chunk), table).astype(BF16)
        gsec_v[rows_c, :] = dot_nt(g_out, w_out_v[...])

    @pl.loop(0, chunks)
    def _(p):
        chunk = chunk_at(p)
        last = p == chunks - 1
        rows_c = rows_of(chunk, size)
        moves = mirror_of(chunk)
        wait_chunk(send_f, recv_f, sf_sem, rf_sem, chunk, last)
        mirrored = dot_tn(moves, recv_f[rows_c, :]).astype(BF16)
        pre_act = local_v[rows_c, :] + dot_nn(mirrored, w_up_v[...])
        q_one = sigmoid(pre_act)
        first_res = (msg_v[rows_c, :].astype(F32) + pre_act * q_one).astype(BF16)
        pre_two = dot_nn(first_res, w_mlp_v[...])
        q_two = sigmoid(pre_two)
        second_v[rows_c, :] = (first_res.astype(F32) + pre_two * q_two).astype(BF16)
        g_second = gsec_v[rows_c, :]
        g_pre2 = (g_second * (q_two * (1.0 + pre_two * (1.0 - q_two)))).astype(BF16)
        g_first = g_second + dot_nt(g_pre2, w_mlp_v[...])
        g_pre = (g_first * (q_one * (1.0 + pre_act * (1.0 - q_one)))).astype(BF16)
        g_mirrored = dot_nt(g_pre, w_up_v[...]).astype(BF16)
        send_b[rows_c, :] = dot_nn(moves, g_mirrored).astype(BF16)
        send_chunk(send_b, recv_b, sb_sem, rb_sem, chunk, last)
        local_v[rows_c, :] = g_first
        gpre_v[rows_c, :] = g_pre

    recv_b[own_rows, :] = send_b[own_rows, :]

    atom_acc[...] = jnp.zeros_like(atom_acc)

    @pl.loop(0, chunks)
    def _(p):
        chunk = chunk_at(p)
        rows_c = rows_of(chunk, size)
        out_edge = dot_nn(second_v[rows_c, :], w_out_v[...]).astype(BF16)
        atom_acc[...] += dot_nn(one_hot_of(chunk), out_edge)

    atom_send[...] = atom_acc[...].astype(BF16)

    def atom_copy(off, part, slot):
        peer = lax.rem(col + off, cols)
        return pltpu.make_async_remote_copy(
            src_ref=atom_send.at[rows_of(part, atom_dev)],
            dst_ref=atom_recv.at[rows_of(slot, atom_dev)],
            send_sem=at_ss.at[off],
            recv_sem=at_rs.at[slot],
            device_id=(row, peer),
            device_id_type=MESH,
        )

    for off in range(1, cols):
        atom_copy(off, lax.rem(col + off, cols), col).start()

    @pl.loop(0, chunks)
    def _(p):
        rows_c = rows_of(chunk_at(p), size)
        local_v[rows_c, :] += dot_nt(gpre_v[rows_c, :], w_self_v[...])

    total = atom_acc[rows_of(col, atom_dev), :]
    for off in range(1, cols):
        peer = lax.rem(col + off, cols)
        atom_copy(off, peer, peer).wait_recv()
        total = total + atom_recv[rows_of(peer, atom_dev), :].astype(F32)
    for off in range(1, cols):
        atom_copy(off, lax.rem(col + off, cols), col).wait_send()
    atoms_v[...] = (total * scale).astype(BF16)
    atoms_done = pltpu.make_async_copy(atoms_v, atoms_out, out_sems.at[chunks])
    atoms_done.start()

    def grad_copy(chunk, p):
        rows_c = rows_of(chunk, size)
        return pltpu.make_async_copy(grad_v.at[rows_c], grad_out.at[rows_c], out_sems.at[p])

    @pl.loop(0, chunks)
    def _(p):
        chunk = chunk_at(p)
        rows_c = rows_of(chunk, size)
        wait_chunk(send_b, recv_b, sb_sem, rb_sem, chunk, p == chunks - 1)
        grad_v[rows_c, :] = (local_v[rows_c, :] + dot_nt(recv_b[rows_c, :], w_down_v[...])).astype(BF16)
        grad_copy(chunk, p).start()

    @pl.loop(0, chunks)
    def _(p):
        chunk = chunk_at(p)
        wait_sent(send_f, recv_f, sf_sem, rf_sem, chunk, p == chunks - 1)
        wait_sent(send_b, recv_b, sb_sem, rb_sem, chunk, p == chunks - 1)
        grad_copy(chunk, p).wait()

    atoms_done.wait()


def on_device(messages, counts, targets, mirror, atom_cot, w_self, w_down, w_up, w_mlp, w_out):
    rows = lax.axis_size("row")
    cols = lax.axis_size("col")
    edges, de = messages.shape
    db = w_down.shape[1]
    da = w_out.shape[1]
    block = edges // rows
    group = 1
    while rows % (2 * group) == 0 and 2 * group * block <= 256:
        group *= 2
    chunks = rows // group
    size = group * block
    atom_dev = atom_cot.shape[0]
    scale = (atom_dev * cols / (edges * cols)) ** 0.5
    any_spec = pl.BlockSpec(memory_space=pl.ANY)
    dma = pltpu.SemaphoreType.DMA
    return pl.pallas_call(
        functools.partial(kernel, rows, cols, group, scale),
        out_shape=(
            jax.ShapeDtypeStruct((atom_dev, da), BF16),
            jax.ShapeDtypeStruct((edges, de), BF16),
        ),
        in_specs=[any_spec] * 10,
        out_specs=(any_spec, any_spec),
        scratch_shapes=[
            pltpu.VMEM((edges, de), BF16),
            pltpu.VMEM((chunks, size), jnp.int32),
            pltpu.VMEM((chunks, size), jnp.int32),
            pltpu.SMEM((rows,), jnp.int32),
            pltpu.VMEM((atom_dev * cols, da), BF16),
            pltpu.VMEM(w_self.shape, BF16),
            pltpu.VMEM(w_down.shape, BF16),
            pltpu.VMEM(w_up.shape, BF16),
            pltpu.VMEM(w_mlp.shape, BF16),
            pltpu.VMEM(w_out.shape, BF16),
            pltpu.VMEM((edges, db), BF16),
            pltpu.VMEM((edges, db), BF16),
            pltpu.VMEM((edges, db), BF16),
            pltpu.VMEM((edges, db), BF16),
            pltpu.VMEM((edges, de), F32),
            pltpu.VMEM((edges, de), BF16),
            pltpu.VMEM((edges, de), F32),
            pltpu.VMEM((edges, de), BF16),
            pltpu.VMEM((edges, de), BF16),
            pltpu.VMEM((atom_dev * cols, da), F32),
            pltpu.VMEM((atom_dev * cols, da), BF16),
            pltpu.VMEM((atom_dev * cols, da), BF16),
            pltpu.VMEM((atom_dev, da), BF16),
            dma((10,)),
            dma((chunks + 1,)),
            dma((rows,)),
            dma((rows,)),
            dma((rows,)),
            dma((rows,)),
            dma((cols,)),
            dma((cols,)),
            dma((cols,)),
            dma((cols,)),
        ],
        compiler_params=pltpu.CompilerParams(
            collective_id=0, has_side_effects=True, vmem_limit_bytes=60 * 1024 * 1024
        ),
    )(
        messages, counts, targets.reshape(chunks, size), mirror.reshape(chunks, size), atom_cot,
        w_self, w_down, w_up, w_mlp, w_out,
    )


def solution(mesh):
    return jax.shard_map(
        on_device,
        mesh=mesh,
        in_specs=(
            P(("row", "col"), None),
            P(("row", "col")),
            P(("row", "col")),
            P(("row", "col")),
            P(("row", "col"), None),
            P(),
            P(),
            P(),
            P(),
            P(),
        ),
        out_specs=(P(("row", "col"), None), P(("row", "col"), None)),
        check_vma=False,
    )
```

time: 65.8 us -> 41 us (0.62)
  Pallas kernels: 0 us -> 34.5 us
  matrix products: 21.4 us -> 0 us
  blocking collectives: 12.8 us -> 0 us
  starting transfers between devices: 11.7 us -> 0 us
  waiting for transfers between devices: 6.59 us -> 0 us
  local copies, waits for them, and re-layouts: 11.2 us -> 5.48 us
  other arithmetic: 0.72 us -> 0 us
    pallas_call x0 -> x1, Pallas kernels: none -> 34.5 us  [on_device(): pl.pallas_call(functools.partial(kernel, rows, cols, group, scale), out_s...]
    dot_general x10 -> x0, matrix products: 21.4 us -> none  [the longest x5 11.5 us: times_transposed(): lax.dot_general(left, weight, (((1,), (1,)), ((), ())), preferred_element...]
    all_to_all x2 -> x0, starting transfers between devices: 11.7 us -> none  [the longest x1 7.51 us: on_device(): lax.all_to_all(down, 'row', split_axis=0, concat_axis=0, tiled=True)]
    gather x2 -> x0, local copies, waits for them, and re-layouts: 8.89 us -> none  [the longest x1 4.95 us: on_device(): g_down = jnp.take(returned, rows_mirror, axis=0)]
    psum x1 -> x0, blocking collectives: 8.37 us -> none  [on_device(): lax.psum(group_terms.astype(jnp.bfloat16), 'col').astype(jnp.float32)]
    all_to_all x2 -> x0, waiting for transfers between devices: 6.59 us -> none  [the longest x1 5.61 us: on_device(): lax.all_to_all(down, 'row', split_axis=0, concat_axis=0, tiled=True)]
    all_gather x1 -> x0, blocking collectives: 4.4 us -> none  [on_device(): shard_rows = lax.all_gather(atom_cot, 'col', axis=0, tiled=True)]
    reshape x0 -> x2, local copies, waits for them, and re-layouts: none -> 1.89 us  [the longest x1 1.29 us: on_device(): targets.reshape(chunks, size)]
  transfers between devices with their start and end apart: 2 -> 0, of which waited for: 2 -> 0; matrix products, arithmetic and copies ran while one was open for 14% -> 0% of each run, Pallas kernels for 0% -> 0%
where the time goes in v1:
time: 41 us; the launch traced here: 40.7 us
  Pallas kernels  34.5 us (84%)
  local copies, waits for them, and re-layouts  5.48 us (13%)
  between operations  0.65 us (2%)
    pallas_call x1, Pallas kernels, on_device(): pl.pallas_call(functools.partial(kernel, rows, cols, group, scale), out_s...  34.5 us
    unnamed x4, local copies, waits for them, and re-layouts  3.59 us
    reshape x1, local copies, waits for them, and re-layouts, on_device(): targets.reshape(chunks, size)  1.29 us

profile of v1, /device:TPU:0, one launch (start us, length us, event | category | flops | bytes accessed | tf_op | source)
XLA Modules:
  0.0 40.7 jit_solution(2007164534071053331)
XLA Ops:
  0.6 0.0 copy-start
  0.6 1.3 %reshape.10.targets = s32[4,256]{1,0:T(4,128)} reshape(s32[1024]{0:T(1024)} %param.12) | data formatting | bytes 8192 | tf_op jit(solution)/shard_map/reshape | solution.py:349
  1.9 0.0 copy-done
  1.9 0.6 %reshape.11.mirror = s32[4,256]{1,0:T(4,128)} reshape(s32[1024]{0:T(1024)S(1)} %copy-done) | data formatting | bytes 8192 | tf_op jit(solution)/shard_map/reshape | solution.py:349
  2.5 34.5 %shard_map.113 = (bf16[32,256]{1,0:T(8,128)(2,1)}, bf16[1024,512]{1,0:T(8,128)(2,1)}) custom-call(bf16[1024,512]{1,0:T(8,128)(2,1)} %messages.1, s32[16]{0:T(128)} %counts.1, s32[4,256]{1,0:T(4,128)} %reshape.10.targets, s32[4,256]{1,0:T(4,128)} %reshape.11.mirror, bf16[32,256]{1,0:T(8,128)(2,1)} %cot.1, bf16[512,512]{1,0:T(8,128)(2,1)} %w_self.1, ...), custom_call_target="tpu_custom_call" | custom-call | tf_op jit(solution)/shard_map/pallas_call | solution.py:302
  37.1 1.3 %copy.14 = bf16[32,256]{1,0:T(8,128)(2,1)} copy(bf16[32,256]{1,0:T(8,128)(2,1)} %get-tuple-element.4) | data formatting | bytes 32768
  38.4 2.3 %copy.15 = bf16[1024,512]{1,0:T(8,128)(2,1)} copy(bf16[1024,512]{1,0:T(8,128)(2,1)} %get-tuple-element.5) | data formatting | bytes 2097152
Async XLA Ops:
  0.6 1.3 %copy-start = (s32[1024]{0:T(1024)S(1)}, s32[1024]{0:T(1024)}, u32[]{:S(2)}) copy-start(s32[1024]{0:T(1024)} %param.13) | copy-start | bytes 12292

commit v2 on v1

--- a/solution.py
+++ b/solution.py
@@ -44,10 +44,10 @@
 def kernel(
     rows, cols, group, scale,
     messages, counts, targets, mirror, cot, w_self, w_down, w_up, w_mlp, w_out,
-    atoms_out, grad_out,
+    atoms_v, grad_v,
     msg_v, targets_v, mirror_v, counts_s, cot_all, w_self_v, w_down_v, w_up_v, w_mlp_v, w_out_v,
-    send_f, recv_f, send_b, recv_b, local_v, second_v, gsec_v, gpre_v, grad_v, atom_acc, atom_send, atom_recv, atoms_v,
-    in_sems, out_sems, sf_sem, rf_sem, sb_sem, rb_sem, cot_ss, cot_rs, at_ss, at_rs,
+    send_f, recv_f, send_b, recv_b, local_v, second_v, gsec_v, gpre_v, atom_acc, atom_send, atom_recv,
+    in_sems, sf_sem, rf_sem, sb_sem, rb_sem, cot_ss, cot_rs, at_ss, at_rs,
 ):
     row = lax.axis_index("row")
     col = lax.axis_index("col")
@@ -177,13 +177,13 @@
         for j in range(group):
             bound = jnp.where(lanes // block == j, counts_s[chunk * group + j], bound)
         live = lax.rem(lanes, block) < bound
-        wanted = jnp.where(live, targets_v[pl.ds(chunk, 1), :], -1)
+        wanted = jnp.where(live, targets_v[:, rows_of(chunk, size)], -1)
         ids = lax.broadcasted_iota(jnp.int32, (atom_group, size), 0)
         return jnp.where(ids == wanted, 1.0, 0.0).astype(BF16)
 
     def mirror_of(chunk):
         lanes = lax.broadcasted_iota(jnp.int32, (1, size), 1)
-        wanted = lanes // block * block + mirror_v[pl.ds(chunk, 1), :]
+        wanted = lanes // block * block + mirror_v[:, rows_of(chunk, size)]
         ids = lax.broadcasted_iota(jnp.int32, (size, size), 0)
         return jnp.where(ids == wanted, 1.0, 0.0).astype(BF16)
 
@@ -258,12 +258,6 @@
     for off in range(1, cols):
         atom_copy(off, lax.rem(col + off, cols), col).wait_send()
     atoms_v[...] = (total * scale).astype(BF16)
-    atoms_done = pltpu.make_async_copy(atoms_v, atoms_out, out_sems.at[chunks])
-    atoms_done.start()
-
-    def grad_copy(chunk, p):
-        rows_c = rows_of(chunk, size)
-        return pltpu.make_async_copy(grad_v.at[rows_c], grad_out.at[rows_c], out_sems.at[p])
 
     @pl.loop(0, chunks)
     def _(p):
@@ -271,16 +265,12 @@
         rows_c = rows_of(chunk, size)
         wait_chunk(send_b, recv_b, sb_sem, rb_sem, chunk, p == chunks - 1)
         grad_v[rows_c, :] = (local_v[rows_c, :] + dot_nt(recv_b[rows_c, :], w_down_v[...])).astype(BF16)
-        grad_copy(chunk, p).start()
 
     @pl.loop(0, chunks)
     def _(p):
         chunk = chunk_at(p)
         wait_sent(send_f, recv_f, sf_sem, rf_sem, chunk, p == chunks - 1)
         wait_sent(send_b, recv_b, sb_sem, rb_sem, chunk, p == chunks - 1)
-        grad_copy(chunk, p).wait()
-
-    atoms_done.wait()
 
 
 def on_device(messages, counts, targets, mirror, atom_cot, w_self, w_down, w_up, w_mlp, w_out):
@@ -297,20 +287,18 @@
     size = group * block
     atom_dev = atom_cot.shape[0]
     scale = (atom_dev * cols / (edges * cols)) ** 0.5
-    any_spec = pl.BlockSpec(memory_space=pl.ANY)
+    hbm_spec = pl.BlockSpec(memory_space=pltpu.HBM)
+    vmem_spec = pl.BlockSpec(memory_space=pltpu.VMEM)
     dma = pltpu.SemaphoreType.DMA
     return pl.pallas_call(
         functools.partial(kernel, rows, cols, group, scale),
-        out_shape=(
-            jax.ShapeDtypeStruct((atom_dev, da), BF16),
-            jax.ShapeDtypeStruct((edges, de), BF16),
-        ),
-        in_specs=[any_spec] * 10,
-        out_specs=(any_spec, any_spec),
+        out_shape=(pltpu.VMEM((atom_dev, da), BF16), pltpu.VMEM((edges, de), BF16)),
+        in_specs=[hbm_spec] * 10,
+        out_specs=(vmem_spec, vmem_spec),
         scratch_shapes=[
             pltpu.VMEM((edges, de), BF16),
-            pltpu.VMEM((chunks, size), jnp.int32),
-            pltpu.VMEM((chunks, size), jnp.int32),
+            pltpu.VMEM((1, edges), jnp.int32),
+            pltpu.VMEM((1, edges), jnp.int32),
             pltpu.SMEM((rows,), jnp.int32),
             pltpu.VMEM((atom_dev * cols, da), BF16),
             pltpu.VMEM(w_self.shape, BF16),
@@ -326,13 +314,10 @@
             pltpu.VMEM((edges, de), BF16),
             pltpu.VMEM((edges, de), F32),
             pltpu.VMEM((edges, de), BF16),
-            pltpu.VMEM((edges, de), BF16),
             pltpu.VMEM((atom_dev * cols, da), F32),
             pltpu.VMEM((atom_dev * cols, da), BF16),
             pltpu.VMEM((atom_dev * cols, da), BF16),
-            pltpu.VMEM((atom_dev, da), BF16),
             dma((10,)),
-            dma((chunks + 1,)),
             dma((rows,)),
             dma((rows,)),
             dma((rows,)),
@@ -343,10 +328,10 @@
             dma((cols,)),
         ],
         compiler_params=pltpu.CompilerParams(
-            collective_id=0, has_side_effects=True, vmem_limit_bytes=60 * 1024 * 1024
+            collective_id=0, has_side_effects=True, vmem_limit_bytes=67043328 - 2 * (edges * de + atom_dev * da) - 65536
         ),
     )(
-        messages, counts, targets.reshape(chunks, size), mirror.reshape(chunks, size), atom_cot,
+        messages, counts, targets.reshape(1, edges), mirror.reshape(1, edges), atom_cot,
         w_self, w_down, w_up, w_mlp, w_out,
     )
 

time: 41 us -> 36.4 us (0.89)
  local copies, waits for them, and re-layouts: 5.48 us -> 1.58 us
    unnamed x4 -> x2, local copies, waits for them, and re-layouts: 3.59 us -> 1.58 us
    reshape x2 -> x0, local copies, waits for them, and re-layouts: 1.89 us -> none  [the longest x1 1.29 us: on_device(): targets.reshape(chunks, size)]
    pallas_call x1, Pallas kernels: 34.5 us -> 34.1 us  [on_device(): pl.pallas_call(functools.partial(kernel, rows, cols, group, scale), out_s...]
where the time goes in v2:
time: 36.4 us; the launch traced here: 36.3 us
  Pallas kernels  34.1 us (94%)
  local copies, waits for them, and re-layouts  1.58 us (4%)
  between operations  0.64 us (2%)
    pallas_call x1, Pallas kernels, on_device(): pl.pallas_call(functools.partial(kernel, rows, cols, group, scale), out_s...  34.1 us
    unnamed x2, local copies, waits for them, and re-layouts  1.58 us

profile of v2, /device:TPU:0, one launch (start us, length us, event | category | flops | bytes accessed | tf_op | source)
XLA Modules:
  0.0 36.3 jit_solution(4228729192933129888)
XLA Ops:
  0.6 34.1 %shard_map.113 = (bf16[32,256]{1,0:T(8,128)(2,1)S(1)}, bf16[1024,512]{1,0:T(8,128)(2,1)S(1)}) custom-call(bf16[1024,512]{1,0:T(8,128)(2,1)} %messages.1, s32[16]{0:T(128)} %counts.1, s32[1,1024]{1,0:T(1,128)} %bitcast.2, s32[1,1024]{1,0:T(1,128)} %bitcast.3, bf16[32,256]{1,0:T(8,128)(2,1)} %cot.1, bf16[512,512]{1,0:T(8,128)(2,1)} %w_self.1, ...), custom_call_target="tpu_custom_call" | custom-call | tf_op jit(solution)/shard_map/pallas_call | solution.py:293
  34.7 0.6 %copy.14 = bf16[32,256]{1,0:T(8,128)(2,1)} copy(bf16[32,256]{1,0:T(8,128)(2,1)S(1)} %get-tuple-element.2) | data formatting | bytes 32768
  35.3 1.0 %copy.15 = bf16[1024,512]{1,0:T(8,128)(2,1)} copy(bf16[1024,512]{1,0:T(8,128)(2,1)S(1)} %get-tuple-element.3) | data formatting | bytes 2097152

commit v3 on v2

--- a/solution.py
+++ b/solution.py
@@ -122,25 +122,33 @@
             else:
                 block_copy(src, dst, s_sems, r_sems, other, row, row).wait_send()
 
-    def chunk_at(p):
-        return partner_of(my_chunk, chunks - 1 - p, chunks) if not chunks & (chunks - 1) else partner_of(my_chunk, p + 1, chunks)
+    def picked(p, order):
+        step = order[-1]
+        for place, value in enumerate(order[:-1]):
+            step = jnp.where(p == place, value, step)
+        return step
+
+    def chunk_at(p, order):
+        return partner_of(my_chunk, picked(p, order), chunks)
+
+    far_first = tuple(range(chunks - 1, -1, -1))
+    send_order = (2, 1, 0, 3) if chunks == 4 else far_first
+    work_order = (0, 1, 2, 3) if chunks == 4 else far_first
+    end_order = (0, 1, 2, 3) if chunks == 4 else far_first
 
     loads[0].wait()
     loads[1].wait()
-
-    @pl.loop(0, chunks)
-    def _(p):
-        rows_c = rows_of(chunk_at(p), size)
+    loads[2].wait()
+    pl.semaphore_wait(barrier, rows + cols - 2)
+
+    @pl.loop(0, chunks)
+    def _(p):
+        rows_c = rows_of(chunk_at(p, send_order), size)
         send_f[rows_c, :] = dot_nn(msg_v[rows_c, :], w_down_v[...]).astype(BF16)
+        send_chunk(send_f, recv_f, sf_sem, rf_sem, chunk_at(p, send_order), picked(p, send_order) == 0)
 
     own_rows = rows_of(row, block)
     recv_f[own_rows, :] = send_f[own_rows, :]
-    loads[2].wait()
-    pl.semaphore_wait(barrier, rows + cols - 2)
-
-    @pl.loop(0, chunks)
-    def _(p):
-        send_chunk(send_f, recv_f, sf_sem, rf_sem, chunk_at(p), p == chunks - 1)
 
     def cot_copy(off, owner):
         peer = lax.rem(col + off, cols)
@@ -162,7 +170,7 @@
 
     @pl.loop(0, chunks)
     def _(p):
-        rows_c = rows_of(chunk_at(p), size)
+        rows_c = rows_of(chunk_at(p, send_order), size)
         local_v[rows_c, :] = dot_nn(msg_v[rows_c, :], w_self_v[...])
 
     for off in range(1, cols):
@@ -189,15 +197,15 @@
 
     @pl.loop(0, chunks)
     def _(p):
-        chunk = chunk_at(p)
+        chunk = chunk_at(p, send_order)
         rows_c = rows_of(chunk, size)
         g_out = dot_tn(one_hot_of(chunk), table).astype(BF16)
         gsec_v[rows_c, :] = dot_nt(g_out, w_out_v[...])
 
     @pl.loop(0, chunks)
     def _(p):
-        chunk = chunk_at(p)
-        last = p == chunks - 1
+        chunk = chunk_at(p, work_order)
+        last = picked(p, work_order) == 0
         rows_c = rows_of(chunk, size)
         moves = mirror_of(chunk)
         wait_chunk(send_f, recv_f, sf_sem, rf_sem, chunk, last)
@@ -224,7 +232,7 @@
 
     @pl.loop(0, chunks)
     def _(p):
-        chunk = chunk_at(p)
+        chunk = chunk_at(p, end_order)
         rows_c = rows_of(chunk, size)
         out_edge = dot_nn(second_v[rows_c, :], w_out_v[...]).astype(BF16)
         atom_acc[...] += dot_nn(one_hot_of(chunk), out_edge)
@@ -247,7 +255,7 @@
 
     @pl.loop(0, chunks)
     def _(p):
-        rows_c = rows_of(chunk_at(p), size)
+        rows_c = rows_of(chunk_at(p, end_order), size)
         local_v[rows_c, :] += dot_nt(gpre_v[rows_c, :], w_self_v[...])
 
     total = atom_acc[rows_of(col, atom_dev), :]
@@ -261,16 +269,16 @@
 
     @pl.loop(0, chunks)
     def _(p):
-        chunk = chunk_at(p)
+        chunk = chunk_at(p, end_order)
         rows_c = rows_of(chunk, size)
-        wait_chunk(send_b, recv_b, sb_sem, rb_sem, chunk, p == chunks - 1)
+        wait_chunk(send_b, recv_b, sb_sem, rb_sem, chunk, picked(p, end_order) == 0)
         grad_v[rows_c, :] = (local_v[rows_c, :] + dot_nt(recv_b[rows_c, :], w_down_v[...])).astype(BF16)
 
     @pl.loop(0, chunks)
     def _(p):
-        chunk = chunk_at(p)
-        wait_sent(send_f, recv_f, sf_sem, rf_sem, chunk, p == chunks - 1)
-        wait_sent(send_b, recv_b, sb_sem, rb_sem, chunk, p == chunks - 1)
+        chunk = chunk_at(p, end_order)
+        wait_sent(send_f, recv_f, sf_sem, rf_sem, chunk, picked(p, end_order) == 0)
+        wait_sent(send_b, recv_b, sb_sem, rb_sem, chunk, picked(p, end_order) == 0)
 
 
 def on_device(messages, counts, targets, mirror, atom_cot, w_self, w_down, w_up, w_mlp, w_out):

time: 36.4 us -> 31.5 us (0.87)
  Pallas kernels: 34.1 us -> 29.2 us
    pallas_call x1, Pallas kernels: 34.1 us -> 29.2 us  [on_device(): pl.pallas_call(functools.partial(kernel, rows, cols, group, scale), out_s...]
where the time goes in v3:
time: 31.5 us; the launch traced here: 31.4 us
  Pallas kernels  29.2 us (93%)
  local copies, waits for them, and re-layouts  1.58 us (5%)
  between operations  0.64 us (2%)
    pallas_call x1, Pallas kernels, on_device(): pl.pallas_call(functools.partial(kernel, rows, cols, group, scale), out_s...  29.2 us
    unnamed x2, local copies, waits for them, and re-layouts  1.58 us

profile of v3, /device:TPU:0, one launch (start us, length us, event | category | flops | bytes accessed | tf_op | source)
XLA Modules:
  0.0 31.4 jit_solution(14550938195596713620)
XLA Ops:
  0.6 29.2 %shard_map.113 = (bf16[32,256]{1,0:T(8,128)(2,1)S(1)}, bf16[1024,512]{1,0:T(8,128)(2,1)S(1)}) custom-call(bf16[1024,512]{1,0:T(8,128)(2,1)} %messages.1, s32[16]{0:T(128)} %counts.1, s32[1,1024]{1,0:T(1,128)} %bitcast.2, s32[1,1024]{1,0:T(1,128)} %bitcast.3, bf16[32,256]{1,0:T(8,128)(2,1)} %cot.1, bf16[512,512]{1,0:T(8,128)(2,1)} %w_self.1, ...), custom_call_target="tpu_custom_call" | custom-call | tf_op jit(solution)/shard_map/pallas_call | solution.py:301
  29.8 0.6 %copy.14 = bf16[32,256]{1,0:T(8,128)(2,1)} copy(bf16[32,256]{1,0:T(8,128)(2,1)S(1)} %get-tuple-element.2) | data formatting | bytes 32768
  30.4 1.0 %copy.15 = bf16[1024,512]{1,0:T(8,128)(2,1)} copy(bf16[1024,512]{1,0:T(8,128)(2,1)S(1)} %get-tuple-element.3) | data formatting | bytes 2097152

commit v4 on v3

--- a/solution.py
+++ b/solution.py
@@ -281,6 +281,18 @@
         wait_sent(send_b, recv_b, sb_sem, rb_sem, chunk, picked(p, end_order) == 0)
 
 
+def write_out(pieces, atoms_v, grad_v, atoms_out, grad_out, sems):
+    size = grad_v.shape[0] // pieces
+    copies = [pltpu.make_async_copy(atoms_v, atoms_out, sems.at[pieces])]
+    for i in range(pieces):
+        part = pl.ds(i * size, size)
+        copies.append(pltpu.make_async_copy(grad_v.at[part], grad_out.at[part], sems.at[i]))
+    for copy in copies:
+        copy.start()
+    for copy in copies:
+        copy.wait()
+
+
 def on_device(messages, counts, targets, mirror, atom_cot, w_self, w_down, w_up, w_mlp, w_out):
     rows = lax.axis_size("row")
     cols = lax.axis_size("col")
@@ -298,7 +310,7 @@
     hbm_spec = pl.BlockSpec(memory_space=pltpu.HBM)
     vmem_spec = pl.BlockSpec(memory_space=pltpu.VMEM)
     dma = pltpu.SemaphoreType.DMA
-    return pl.pallas_call(
+    held = pl.pallas_call(
         functools.partial(kernel, rows, cols, group, scale),
         out_shape=(pltpu.VMEM((atom_dev, da), BF16), pltpu.VMEM((edges, de), BF16)),
         in_specs=[hbm_spec] * 10,
@@ -342,6 +354,18 @@
         messages, counts, targets.reshape(1, edges), mirror.reshape(1, edges), atom_cot,
         w_self, w_down, w_up, w_mlp, w_out,
     )
+    pieces = 8
+    return pl.pallas_call(
+        functools.partial(write_out, pieces),
+        out_shape=(
+            jax.ShapeDtypeStruct((atom_dev, da), BF16),
+            jax.ShapeDtypeStruct((edges, de), BF16),
+        ),
+        in_specs=[pl.BlockSpec(memory_space=pl.ANY)] * 2,
+        out_specs=(hbm_spec, hbm_spec),
+        scratch_shapes=[dma((pieces + 1,))],
+        compiler_params=pltpu.CompilerParams(vmem_limit_bytes=256 * 1024),
+    )(*held)
 
 
 def solution(mesh):

time: 31.5 us -> 31 us (0.984)
  local copies, waits for them, and re-layouts: 1.58 us -> 0 us
  Pallas kernels: 29.2 us -> 30.2 us
    unnamed x2 -> x0, local copies, waits for them, and re-layouts: 1.58 us -> none
    pallas_call x0 -> x1, Pallas kernels: none -> 1.04 us  [on_device(): pl.pallas_call(functools.partial(write_out, pieces), out_shape=(jax.Shape...]
where the time goes in v4:
time: 31 us; the launch traced here: 30.8 us
  Pallas kernels  30.2 us (97%)
  between operations  0.64 us (2%)
    pallas_call x1, Pallas kernels, on_device(): pl.pallas_call(functools.partial(kernel, rows, cols, group, scale), out_s...  29.2 us
    pallas_call x1, Pallas kernels, on_device(): pl.pallas_call(functools.partial(write_out, pieces), out_shape=(jax.Shape...  1.04 us

profile of v4, /device:TPU:0, one launch (start us, length us, event | category | flops | bytes accessed | tf_op | source)
XLA Modules:
  0.0 30.8 jit_solution(11982607947306151256)
XLA Ops:
  0.6 29.2 %shard_map.113 = (bf16[32,256]{1,0:T(8,128)(2,1)S(1)}, bf16[1024,512]{1,0:T(8,128)(2,1)S(1)}) custom-call(bf16[1024,512]{1,0:T(8,128)(2,1)} %messages.1, s32[16]{0:T(128)} %counts.1, s32[1,1024]{1,0:T(1,128)} %bitcast.2, s32[1,1024]{1,0:T(1,128)} %bitcast.3, bf16[32,256]{1,0:T(8,128)(2,1)} %cot.1, bf16[512,512]{1,0:T(8,128)(2,1)} %w_self.1, ...), custom_call_target="tpu_custom_call" | custom-call | tf_op jit(solution)/shard_map/pallas_call | solution.py:313
  29.8 1.0 %shard_map.114 = (bf16[32,256]{1,0:T(8,128)(2,1)}, bf16[1024,512]{1,0:T(8,128)(2,1)}) custom-call(bf16[32,256]{1,0:T(8,128)(2,1)S(1)} %get-tuple-element.4.atoms_v, bf16[1024,512]{1,0:T(8,128)(2,1)S(1)} %get-tuple-element.5.grad_v), custom_call_target="tpu_custom_call" | custom-call | tf_op jit(solution)/shard_map/pallas_call | solution.py:358
